TPU v7x, 128 devices: a whole 4x4x4 slice. The times are simulated.
128 devices in a mesh: tok: 8 (over x, core), head: 8 (over y, z_hi), seq: 2 (over z_lo).
Axes of the slice: x: 4, y: 4, z: 4 (z_hi: 2, z_lo: 2; z = z_hi * 2 + z_lo), core: 2. Of those that a mesh axis runs over, the one named last changes fastest.
Arguments:
- queries: bfloat16 [2, 8192, 4096], P('seq', ('tok', 'head')), may hold values from -6 to 6
- keys: bfloat16 [2, 8192, 4096], P('seq', ('tok', 'head')), may hold values from -6 to 6
- values: bfloat16 [2, 8192, 4096], P('seq', ('tok', 'head')), may hold values from -6 to 6
- rates: float32 [2, 8, 8192], P('seq', 'head', 'tok'), may hold values from 0.00011048543 to 0.0011048544
- fast_one: float32 [8, 512, 512], P('head'), may hold values from -0.25 to 0.25
- fast_two: float32 [8, 512, 512], P('head'), may hold values from -0.25 to 0.25
- fast_three: float32 [8, 512, 512], P('head'), may hold values from -0.25 to 0.25
- grad_out: bfloat16 [2, 8192, 4096], P('seq', ('tok', 'head')), may hold values from -6 to 6
Outputs:
- grad_queries: bfloat16 [2, 8192, 4096], P('seq', ('tok', 'head'))
- grad_keys: bfloat16 [2, 8192, 4096], P('seq', ('tok', 'head'))
- grad_values: bfloat16 [2, 8192, 4096], P('seq', ('tok', 'head'))
- grad_rates: float32 [2, 8, 8192], P('seq', 'head', 'tok')
- grad_fast_one: float32 [8, 512, 512], P('head')
- grad_fast_two: float32 [8, 512, 512], P('head')
- grad_fast_three: float32 [8, 512, 512], P('head')
All inputs are finite; a program needn't handle non-finite values.
Results may differ from a plain program's by a relative error of at most 0.016.
Values may be sent and summed in bfloat16 or wider, within the bound.
A program may use at most 128 MiB of HBM per device.

v0:
```python
import jax
import jax.numpy as jnp
from jax import lax
from jax.sharding import PartitionSpec as P

epsilon = 1e-06


def side_by_side(arrays, axis, split_dim, concat_dim, along):
    ends, at = ([], 0)
    for a in arrays[:-1]:
        at += a.shape[along]
        ends.append(at)
    both = jnp.concatenate(arrays, axis=along)
    return tuple(
        jnp.split(
            lax.all_to_all(both, axis, split_axis=split_dim, concat_axis=concat_dim, tiled=True),
            ends,
            axis=along,
        )
    )


def shortened(value):

    def short(part):
        return part.astype(jnp.bfloat16) if part.dtype == jnp.float32 else part

    return jax.tree.map(short, value)


def matmul(left, right):
    return jnp.dot(
        left.astype(jnp.bfloat16), right.astype(jnp.bfloat16), preferred_element_type=jnp.float32
    )


def matmul_tn(left, right):
    return lax.dot_general(
        left.astype(jnp.bfloat16),
        right.astype(jnp.bfloat16),
        (((0,), (0,)), ((), ())),
        preferred_element_type=jnp.float32,
    )


def matmul_nt(left, right):
    return lax.dot_general(
        left.astype(jnp.bfloat16),
        right.astype(jnp.bfloat16),
        (((1,), (1,)), ((), ())),
        preferred_element_type=jnp.float32,
    )


def activation(preact):
    squash = jax.nn.sigmoid(preact)
    swished = preact * squash
    slope_one = squash * (1.0 + preact * (1.0 - squash))
    slope_two = squash * (1.0 - squash) * (2.0 + preact * (1.0 - 2.0 * squash))
    return (squash, swished, slope_one, slope_two)


def inner_forward(keys_h, values_h, rate_h, w_one, w_two, w_three):
    pre_one = matmul(keys_h, w_one)
    pre_three = matmul(keys_h, w_three)
    parts = activation(pre_one)
    swished, slope_one = (parts[1], parts[2])
    hidden = swished * pre_three
    target = -rate_h[:, None] * values_h.astype(jnp.float32)
    grad_two = matmul_tn(hidden, target)
    back_hidden = matmul_nt(target, w_two)
    delta_one = back_hidden * pre_three * slope_one
    delta_three = back_hidden * swished
    grad_one = matmul_tn(keys_h, delta_one)
    grad_three = matmul_tn(keys_h, delta_three)
    saved = (pre_one, pre_three, target, back_hidden, delta_one, delta_three)
    return ((grad_one, grad_two, grad_three), saved)


def normalize(weight, update):
    ref_norm = jnp.sqrt(jnp.sum(weight * weight, axis=-2, keepdims=True) + epsilon)
    upd_norm = jnp.sqrt(jnp.sum(update * update, axis=-2, keepdims=True) + epsilon)
    return (update * (ref_norm / upd_norm), ref_norm, upd_norm)


def apply_backward(queries_h, cotangent, new_one, new_two, new_three):
    pre_one = matmul(queries_h, new_one)
    pre_three = matmul(queries_h, new_three)
    parts = activation(pre_one)
    swished, slope_one = (parts[1], parts[2])
    hidden = swished * pre_three
    grad_two = matmul_tn(hidden, cotangent)
    back_hidden = matmul_nt(cotangent, new_two)
    delta_one = back_hidden * pre_three * slope_one
    delta_three = back_hidden * swished
    grad_one = matmul_tn(queries_h, delta_one)
    grad_three = matmul_tn(queries_h, delta_three)
    grad_queries = matmul_nt(delta_one, new_one) + matmul_nt(delta_three, new_three)
    return ((grad_one, grad_two, grad_three), grad_queries)


def adjoint(weight, update, ref_norm, upd_norm, grad_new):
    moment = jnp.sum(grad_new * update, axis=-2, keepdims=True)
    factor = ref_norm / upd_norm
    grad_update = factor * grad_new - update * (factor * moment / (upd_norm * upd_norm))
    direct = weight * (moment / (upd_norm * ref_norm)) + grad_update
    return (-grad_update, direct)


def double_backward(
    keys_h, values_h, rate_h, w_one, w_two, w_three, saved, cot_one, cot_two, cot_three
):
    pre_one, pre_three, target, back_hidden, delta_one, delta_three = saved
    parts = activation(pre_one)
    swished, slope_one, slope_two = (parts[1], parts[2], parts[3])
    hidden = swished * pre_three
    grad_hidden = matmul_nt(target, cot_two)
    grad_target = matmul(hidden, cot_two)
    grad_delta_one = matmul(keys_h, cot_one)
    grad_delta_three = matmul(keys_h, cot_three)
    grad_keys = matmul_nt(delta_one, cot_one) + matmul_nt(delta_three, cot_three)
    grad_back = grad_delta_one * pre_three * slope_one + grad_delta_three * swished
    grad_pre_three = grad_delta_one * back_hidden * slope_one + grad_hidden * swished
    grad_pre_one = (
        grad_delta_one * back_hidden * pre_three * slope_two
        + grad_delta_three * back_hidden * slope_one
        + grad_hidden * pre_three * slope_one
    )
    grad_target = grad_target + matmul(grad_back, w_two)
    weight_two = matmul_tn(grad_back, target)
    grad_keys = grad_keys + (matmul_nt(grad_pre_one, w_one) + matmul_nt(grad_pre_three, w_three))
    weight_one = matmul_tn(keys_h, grad_pre_one)
    weight_three = matmul_tn(keys_h, grad_pre_three)
    grad_values = -rate_h[:, None] * grad_target
    grad_rate = -jnp.sum(values_h.astype(jnp.float32) * grad_target, axis=1)
    return (grad_keys, grad_values, grad_rate, (weight_one, weight_two, weight_three))


def body(queries, keys, values, rates, fast_one, fast_two, fast_three, grad_out):
    heads = fast_one.shape[0]
    width = fast_one.shape[1]
    weights = (fast_one, fast_two, fast_three)
    key_local, value_local = side_by_side((keys, values), "head", 2, 1, 0)
    inner_list, saved_list = ([], [])
    head_idx = 0
    start = head_idx * width
    inner, saved = inner_forward(
        key_local[0, :, start : start + width],
        value_local[0, :, start : start + width],
        rates[0, head_idx],
        fast_one[head_idx],
        fast_two[head_idx],
        fast_three[head_idx],
    )
    inner_list.append(inner)
    saved_list.append(saved)
    partial_inner = tuple((jnp.stack([inner_list[0][index]]) for index in range(3)))
    summed_inner = lax.psum(partial_inner, "tok")
    query_local, cot_local = side_by_side((queries, grad_out), "head", 2, 1, 0)
    updates = [weights[index] - summed_inner[index] for index in range(3)]
    normed = [normalize(weights[index], updates[index]) for index in range(3)]
    new_list, query_heads = ([], [])
    head_idx = 0
    start = head_idx * width
    grads_new, grad_queries = apply_backward(
        query_local[0, :, start : start + width],
        cot_local[0, :, start : start + width],
        normed[0][0][head_idx],
        normed[1][0][head_idx],
        normed[2][0][head_idx],
    )
    new_list.append(grads_new)
    query_heads.append(grad_queries)
    partial_new = tuple((jnp.stack([new_list[0][index]]) for index in range(3)))
    query_block = query_heads[0].astype(jnp.bfloat16)[None]
    query_back = lax.all_to_all(query_block, "head", split_axis=1, concat_axis=2, tiled=True)
    summed_new = lax.psum(partial_new, "tok")
    keep_flag = (lax.axis_index("tok") == 0).astype(jnp.float32)
    results = [
        adjoint(
            weights[index], updates[index], normed[index][1], normed[index][2], summed_new[index]
        )
        for index in range(3)
    ]
    cotangents = [results[index][0] for index in range(3)]
    directs = [results[index][1] * keep_flag for index in range(3)]
    key_heads, value_heads, rate_heads, extra_list = ([], [], [], [])
    head_idx = 0
    start = head_idx * width
    grad_keys, grad_values, grad_rate, extra = double_backward(
        key_local[0, :, start : start + width],
        value_local[0, :, start : start + width],
        rates[0, head_idx],
        fast_one[head_idx],
        fast_two[head_idx],
        fast_three[head_idx],
        saved_list[head_idx],
        cotangents[0][head_idx],
        cotangents[1][head_idx],
        cotangents[2][head_idx],
    )
    key_heads.append(grad_keys.astype(jnp.bfloat16))
    value_heads.append(grad_values.astype(jnp.bfloat16))
    rate_heads.append(grad_rate)
    extra_list.append(extra)
    partial_weights = tuple(
        (directs[index] + jnp.stack([extra_list[0][index]]) for index in range(3))
    )
    total_one, total_two, total_three = jax.tree.map(
        lambda part: part.astype(jnp.float32), lax.psum(shortened(partial_weights), ("tok", "seq"))
    )
    key_block = key_heads[0][None]
    value_block = value_heads[0][None]
    key_back, value_back = side_by_side((key_block, value_block), "head", 1, 2, 0)
    rate_grads = jnp.stack(rate_heads)[None]
    return (query_back, key_back, value_back, rate_grads, total_one, total_two, total_three)


def solution(mesh):
    placed = (
        P("seq", ("tok", "head"), None),
        P("seq", ("tok", "head"), None),
        P("seq", ("tok", "head"), None),
        P("seq", "head", "tok"),
        P("head", None, None),
        P("head", None, None),
        P("head", None, None),
        P("seq", ("tok", "head"), None),
    )
    return jax.shard_map(
        body,
        mesh=mesh,
        in_specs=placed,
        out_specs=(
            P("seq", ("tok", "head"), None),
            P("seq", ("tok", "head"), None),
            P("seq", ("tok", "head"), None),
            P("seq", "head", "tok"),
            P("head", None, None),
            P("head", None, None),
            P("head", None, None),
        ),
        check_vma=False,
    )
```

profile of v0, /device:TPU:1, one launch (start us, length us, event | category | flops | bytes accessed | tf_op | source)
XLA Modules:
  0.0 484.2 jit_solution(5529471393245594606)
XLA Ops:
  7.2 1.7 pad_maximum_fusion.1
  8.9 3.8 copy.86
  12.7 8.5 %all-to-all-start.1 = ((bf16[2,128,4096]{1,0,2:T(2,128)(2,1)}), bf16[2,128,4096]{1,0,2:T(2,128)(2,1)}, u32[]{:S(2)}, u32[]{:S(2)}) async-start(bf16[2,128,4096]{1,0,2:T(2,128)(2,1)} %copy.86), calls=%async_computation.1 | async-start | bytes 4194304 | tf_op jit(solution)/shard_map/all_to_all | solution.py:17
  21.2 2.8 copy.82
  24.0 5.5 %copy.83 = bf16[1,128,4096]{1,0,2:T(2,128)(2,1)} copy(bf16[1,128,4096]{2,1,0:T(8,128)(2,1)} %param.15) | data formatting | bytes 2097152 | tf_op args[7]
  29.5 6.4 %pad_maximum_fusion = bf16[2,128,4096]{1,0,2:T(2,128)(2,1)} fusion(bf16[1,128,4096]{1,0,2:T(2,128)(2,1)} %copy.83, bf16[1,128,4096]{1,0,2:T(2,128)(2,1)S(1)} %copy.82), kind=kLoop, calls=%fused_computation.9 | loop fusion | flops 4194304 | bytes 4194304 | tf_op jit(solution)/shard_map/concatenate | solution.py:14
  35.9 15.9 %all-to-all-done.1 = bf16[2,128,4096]{1,0,2:T(2,128)(2,1)} async-done(((bf16[2,128,4096]{1,0,2:T(2,128)(2,1)}), bf16[2,128,4096]{1,0,2:T(2,128)(2,1)}, u32[]{:S(2)}, u32[]{:S(2)}) %all-to-all-start.1) | async-done | bytes 2097184 | tf_op jit(solution)/shard_map/all_to_all | solution.py:17
  51.9 4.4 all-to-all-start
  56.3 4.7 copy.87
  61.1 1.9 copy-done.2
  65.6 1.4 copy-done.13
  66.9 3.1 multiply_convert_fusion.5
  70.1 1.7 convolution_bitcast_fusion.6
  73.1 1.7 convolution_bitcast_fusion.8
  74.9 11.2 %all-to-all-done = bf16[2,128,4096]{1,0,2:T(2,128)(2,1)} async-done(((bf16[2,128,4096]{1,0,2:T(2,128)(2,1)}), bf16[2,128,4096]{1,0,2:T(2,128)(2,1)}, u32[]{:S(2)}, u32[]{:S(2)}) %all-to-all-start) | async-done | bytes 2097184 | tf_op jit(solution)/shard_map/all_to_all | solution.py:17
  86.0 1.9 copy.84
  90.7 3.0 convolution_bitcast_fusion.7
  93.7 47.7 %all-reduce.13.cloned.1.call-done = (f32[1,512,512]{2,1,0:T(8,128)}, f32[1,512,512]{2,1,0:T(8,128)}) async-done(((f32[1,512,512]{2,1,0:T(8,128)}, f32[1,512,512]{2,1,0:T(8,128)}), (f32[1,512,512]{2,1,0:T(8,128)}, f32[1,512,512]{2,1,0:T(8,128)})) %all-reduce.13.cloned.1.call-update) | async-done | bytes 2097168 | tf_op jit(solution)/shard_map/psum | solution.py:159
  141.4 2.5 multiply_reduce_fusion.3
  145.5 2.3 multiply_convert_fusion.2
  148.8 1.7 convolution_bitcast_fusion.4
  151.1 65.1 %all-reduce.11.cloned.1.call-done = (f32[1,512,512]{2,1,0:T(8,128)}, f32[1,512,512]{2,1,0:T(8,128)}) async-done(((f32[1,512,512]{2,1,0:T(8,128)}, f32[1,512,512]{2,1,0:T(8,128)}), (f32[1,512,512]{2,1,0:T(8,128)}, f32[1,512,512]{2,1,0:T(8,128)})) %all-reduce.11.cloned.1.call-update) | async-done | bytes 2097168 | tf_op jit(solution)/shard_map/psum | solution.py:159
  216.1 2.4 multiply_reduce_fusion.1
  219.0 2.8 multiply_convert_fusion.3
  221.8 1.7 convolution_bitcast_fusion.5
  223.5 2.1 fusion.47
  225.6 1.8 convolution_bitcast_fusion.3
  227.5 2.7 fusion.12
  230.1 3.0 copy.101
  233.6 9.0 %reduce.9 = bf16[1024,512]{1,0:T(8,128)(2,1)} reduce(bf16[1024,1,512]{2,1,0:T(2,128)(2,1)} %bitcast.164, bf16[]{:T(256)} %broadcast.129), dimensions={1}, to_apply=%bitcast.149.reduce_sub_computation | reduce | bytes 2097154
  242.6 2.8 reshape.255
  245.4 6.6 %all-to-all-start.2 = ((bf16[8,2,32768]{2,1,0:T(2,128)(2,1)}), bf16[8,2,32768]{2,1,0:T(2,128)(2,1)}, u32[]{:S(2)}, u32[]{:S(2)}) async-start(bf16[8,2,32768]{2,1,0:T(2,128)(2,1)} %reshape.255), calls=%async_computation.2 | async-start | bytes 2097152 | tf_op jit(solution)/shard_map/all_to_all | solution.py:177
  252.0 1.5 fusion.27
  253.6 2.1 fusion.62
  255.6 2.1 fusion.60
  257.7 35.6 %all-reduce.9.cloned.1.call-done = (f32[1,512,512]{2,1,0:T(8,128)}, f32[1,512,512]{2,1,0:T(8,128)}) async-done(((f32[1,512,512]{2,1,0:T(8,128)}, f32[1,512,512]{2,1,0:T(8,128)}), (f32[1,512,512]{2,1,0:T(8,128)}, f32[1,512,512]{2,1,0:T(8,128)})) %all-reduce.9.cloned.1.call-update) | async-done | bytes 2097168 | tf_op jit(solution)/shard_map/psum | solution.py:178
  293.3 1.5 multiply_reduce_fusion.2
  301.6 2.7 add_convert_fusion.2
  309.6 3.5 copy.93
  313.2 1.6 fusion.17
  314.8 1.6 fusion.18
  316.4 6.7 %all-to-all-start.3 = ((bf16[2,1024,512]{2,0,1:T(2,128)(2,1)}), bf16[2,1024,512]{2,0,1:T(2,128)(2,1)}, u32[]{:S(2)}, u32[]{:S(2)}) async-start(bf16[2,1024,512]{2,0,1:T(2,128)(2,1)} %copy.93), calls=%async_computation.3 | async-start | bytes 4194304 | tf_op jit(solution)/shard_map/all_to_all | solution.py:17
  323.2 3.1 fusion.19
  326.4 4.5 reshape.256
  333.8 127.8 %all-reduce.15.cloned.1.call-done = (bf16[1,512,512]{2,1,0:T(8,128)(2,1)}, bf16[1,512,512]{2,1,0:T(8,128)(2,1)}, bf16[1,512,512]{2,1,0:T(8,128)(2,1)}) async-done(((bf16[1,512,512]{2,1,0:T(8,128)(2,1)}, bf16[1,512,512]{2,1,0:T(8,128)(2,1)}, bf16[1,512,512]{2,1,0:T(8,128)(2,1)}), (bf16[1,512,512]{2,1,0:T(8,128)(2,1)}, bf16[1,512,512]{2,1,0:T(8,128)(2,1)}, ...) | async-done | bytes 1572880 | tf_op jit(solution)/shard_map/psum | solution.py:211
  461.6 2.2 convert_element_type.196
  463.8 2.1 convert_element_type.198
  467.1 5.5 %fusion.55 = (bf16[1,128,8,512]{3,0,1,2:T(2,128)(2,1)S(1)}, bf16[1,128,8,512]{3,0,1,2:T(2,128)(2,1)S(1)}) fusion(bf16[2,128,8,512]{3,0,1,2:T(2,128)(2,1)} %bitcast.33), kind=kLoop, calls=%fused_computation.110 | loop fusion | bytes 4194304 | tf_op jit(solution)/shard_map/split | solution.py:16
  (127 shorter events, 31.7 us)
Async XLA Ops:
  12.7 8.5 %copy-start.40 = (f32[1,1,1024]{2,1,0:T(1,128)S(1)}, f32[1,1,1024]{2,1,0:T(1,128)}, u32[]{:S(2)}) copy-start(f32[1,1,1024]{2,1,0:T(1,128)} %param.11) | copy-start | bytes 12292
  12.7 8.5 %copy-start.28 = (bf16[1,128,4096]{2,1,0:T(8,128)(2,1)S(1)}, bf16[1,128,4096]{2,1,0:T(8,128)(2,1)}, u32[]{:S(2)}) copy-start(bf16[1,128,4096]{2,1,0:T(8,128)(2,1)} %param.8) | copy-start | bytes 3145732
  12.7 39.2 %all-to-all-start.1 = ((bf16[2,128,4096]{1,0,2:T(2,128)(2,1)}), bf16[2,128,4096]{1,0,2:T(2,128)(2,1)}, u32[]{:S(2)}, u32[]{:S(2)}) async-start(bf16[2,128,4096]{1,0,2:T(2,128)(2,1)} %copy.86), calls=%async_computation.1 | async-start | bytes 4194304 | tf_op jit(solution)/shard_map/all_to_all | solution.py:17
  51.9 34.2 %all-to-all-start = ((bf16[2,128,4096]{1,0,2:T(2,128)(2,1)}), bf16[2,128,4096]{1,0,2:T(2,128)(2,1)}, u32[]{:S(2)}, u32[]{:S(2)}) async-start(bf16[2,128,4096]{1,0,2:T(2,128)(2,1)} %pad_maximum_fusion), calls=%async_computation | async-start | bytes 4194304 | tf_op jit(solution)/shard_map/all_to_all | solution.py:17
  56.2 85.2 %all-reduce.13.cloned.1.call-start = ((), (), s32[]{:S(2)}) async-start(), calls=%async_computation.6 | async-start | bytes 4194304 | tf_op jit(solution)/shard_map/psum | solution.py:159
  61.0 10.8 %copy-start = (bf16[2,128,8,512]{3,1,2,0:T(8,128)(2,1)}, bf16[2,128,8,512]{3,1,2,0:T(8,128)(2,1)S(1)}, u32[]{:S(2)}) copy-start(bf16[2,128,8,512]{3,1,2,0:T(8,128)(2,1)S(1)} %copy.87) | copy-start | bytes 6291460
  61.0 2.0 copy-start.2
  63.0 1.2 copy-start.6
  64.2 1.4 copy-start.22
  64.9 5.2 %copy-start.24 = (f32[1024,512]{1,0:T(8,128)}, f32[1024,512]{1,0:T(8,128)S(1)}, u32[]{:S(2)}) copy-start(f32[1024,512]{1,0:T(8,128)S(1)} %fusion.37) | copy-start | bytes 6291460
  64.9 2.0 copy-start.13
  65.3 4.8 copy-start.35
  70.1 1.7 copy-start.31
  70.1 2.0 copy-start.29
  72.1 1.0 copy-start.16
  74.8 141.3 %all-reduce.11.cloned.1.call-start = ((), (), s32[]{:S(2)}) async-start(), calls=%async_computation.5 | async-start | bytes 4194304 | tf_op jit(solution)/shard_map/psum | solution.py:159
  90.7 50.8 %copy-start.7 = (f32[1,512,512]{2,1,0:T(8,128)S(1)}, f32[1,512,512]{2,1,0:T(8,128)}, u32[]{:S(2)}) copy-start(f32[1,512,512]{2,1,0:T(8,128)} %param.12) | copy-start | bytes 3145732
  141.4 2.5 copy-start.19
  143.9 1.0 copy-start.4
  144.0 1.6 copy-start.37
  144.7 3.1 copy-start.26
  150.5 142.7 %all-reduce.9.cloned.1.call-start = ((), (), s32[]{:S(2)}) async-start(), calls=%async_computation.4 | async-start | bytes 4194304 | tf_op jit(solution)/shard_map/psum | solution.py:178
  216.1 2.4 copy-start.20
  216.1 2.9 copy-start.27
  223.5 2.1 copy-start.38
  245.4 71.0 %all-to-all-start.2 = ((bf16[8,2,32768]{2,1,0:T(2,128)(2,1)}), bf16[8,2,32768]{2,1,0:T(2,128)(2,1)}, u32[]{:S(2)}, u32[]{:S(2)}) async-start(bf16[8,2,32768]{2,1,0:T(2,128)(2,1)} %reshape.255), calls=%async_computation.2 | async-start | bytes 2097152 | tf_op jit(solution)/shard_map/all_to_all | solution.py:177
  253.5 2.1 copy-start.33
  293.3 1.5 copy-start.11
  295.1 1.2 copy-start.32
  295.1 4.7 copy-start.41
  296.3 1.2 copy-start.5
  296.3 1.5 copy-start.12
  297.9 1.2 copy-start.30
  297.9 1.9 copy-start.36
  298.2 1.9 copy-start.23
  298.2 2.5 copy-start.25
  299.1 2.5 copy-start.21
  301.6 2.7 copy-start.8
  304.3 2.0 copy-start.1
  304.3 2.2 copy-start.14
  306.6 1.2 copy-start.3
  306.6 1.9 copy-start.15
  309.6 3.5 copy-start.10
  313.2 1.7 copy-start.17
  316.4 6.8 %copy-start.9 = (f32[1,512,512]{2,1,0:T(8,128)S(1)}, f32[1,512,512]{2,1,0:T(8,128)}, u32[]{:S(2)}) copy-start(f32[1,512,512]{2,1,0:T(8,128)} %param.12) | copy-start | bytes 3145732
  316.4 150.6 %all-to-all-start.3 = ((bf16[2,1024,512]{2,0,1:T(2,128)(2,1)}), bf16[2,1024,512]{2,0,1:T(2,128)(2,1)}, u32[]{:S(2)}, u32[]{:S(2)}) async-start(bf16[2,1024,512]{2,0,1:T(2,128)(2,1)} %copy.93), calls=%async_computation.3 | async-start | bytes 4194304 | tf_op jit(solution)/shard_map/all_to_all | solution.py:17
  323.2 138.4 %all-reduce.15.cloned.1.call-start = ((), (), s32[]{:S(2)}) async-start(), calls=%async_computation.7 | async-start | bytes 3145728 | tf_op jit(solution)/shard_map/psum | solution.py:211
  461.6 4.4 copy-start.39
  (2 other events, 1.9 us)
Sparse Core Ops, SparseCore 0:
  74.9 66.4 all-reduce.12
  150.7 65.4 all-reduce.10
  227.6 65.6 all-reduce.8
  326.9 134.6 all-reduce.14
where the time goes:
time: 493 us; the launch traced here: 484 us
  waiting for transfers between devices  303 us (61%)
  local copies, waits for them, and re-layouts  62.1 us (13%)
  matrix products  44.9 us (9%)
  other arithmetic  32.7 us (7%)
  starting transfers between devices  26.8 us (5%)
  between operations  14.5 us (3%)
    psum x1, waiting for transfers between devices, body(): lax.psum(shortened(partial_weights), ('tok', 'seq'))  128 us
    psum x2, waiting for transfers between devices, body(): summed_inner = lax.psum(partial_inner, 'tok')  113 us
    psum x1, waiting for transfers between devices, body(): summed_new = lax.psum(partial_new, 'tok')  35.6 us
    unnamed x91, local copies, waits for them, and re-layouts  31.3 us
    all_to_all x3, waiting for transfers between devices, side_by_side(): lax.all_to_all(both, axis, split_axis=split_dim, concat_axis=concat_dim,...  27.1 us
    all_to_all x3, starting transfers between devices, side_by_side(): lax.all_to_all(both, axis, split_axis=split_dim, concat_axis=concat_dim,...  19.5 us
    dot_general x9, matrix products, matmul_tn(): lax.dot_general(left.astype(jnp.bfloat16), right.astype(jnp.bfloat16), ((...  18.1 us
    dot_general x9, matrix products, matmul_nt(): lax.dot_general(left.astype(jnp.bfloat16), right.astype(jnp.bfloat16), ((...  17.5 us
  transfers between devices with their start and end apart: 8, of which 6 were waited for; matrix products, arithmetic and copies ran while one was open for 19% of the time, Pallas kernels for 0%

commit v1 on v0

--- a/solution.py
+++ b/solution.py
@@ -208,7 +208,8 @@
         (directs[index] + jnp.stack([extra_list[0][index]]) for index in range(3))
     )
     total_one, total_two, total_three = jax.tree.map(
-        lambda part: part.astype(jnp.float32), lax.psum(shortened(partial_weights), ("tok", "seq"))
+        lambda part: part.astype(jnp.float32),
+        lax.psum(lax.psum(shortened(partial_weights), "tok"), "seq"),
     )
     key_block = key_heads[0][None]
     value_block = value_heads[0][None]

time: 493 us -> 475 us (0.963)
  waiting for transfers between devices: 303 us -> 284 us
    psum x1 -> x2, waiting for transfers between devices: 128 us -> 109 us  [the longest x1 64.3 us: body(): lax.psum(shortened(partial_weights), 'tok')]
    unnamed x91 -> x97, local copies, waits for them, and re-layouts: 31.3 us -> 31.7 us
  transfers between devices with their start and end apart: 8 -> 9, of which waited for: 6 -> 7; matrix products, arithmetic and copies ran while one was open for 19% -> 21% of each run, Pallas kernels for 0% -> 0%
where the time goes in v1:
time: 475 us; the launch traced here: 466 us
  waiting for transfers between devices  284 us (60%)
  local copies, waits for them, and re-layouts  62.6 us (13%)
  matrix products  45.5 us (10%)
  other arithmetic  32.7 us (7%)
  starting transfers between devices  26.8 us (6%)
  between operations  14.5 us (3%)
    psum x2, waiting for transfers between devices, body(): summed_inner = lax.psum(partial_inner, 'tok')  113 us
    psum x1, waiting for transfers between devices, body(): lax.psum(shortened(partial_weights), 'tok')  64.3 us
    psum x1, waiting for transfers between devices, body(): lax.psum(lax.psum(shortened(partial_weights), 'tok'), 'seq')  44.2 us
    psum x1, waiting for transfers between devices, body(): summed_new = lax.psum(partial_new, 'tok')  35.6 us
    unnamed x97, local copies, waits for them, and re-layouts  31.7 us
    all_to_all x3, waiting for transfers between devices, side_by_side(): lax.all_to_all(both, axis, split_axis=split_dim, concat_axis=concat_dim,...  27.1 us
    all_to_all x3, starting transfers between devices, side_by_side(): lax.all_to_all(both, axis, split_axis=split_dim, concat_axis=concat_dim,...  19.6 us
    dot_general x9, matrix products, matmul_tn(): lax.dot_general(left.astype(jnp.bfloat16), right.astype(jnp.bfloat16), ((...  18.9 us
  transfers between devices with their start and end apart: 9, of which 7 were waited for; matrix products, arithmetic and copies ran while one was open for 21% of the time, Pallas kernels for 0%

profile of v1, /device:TPU:1, one launch (start us, length us, event | category | flops | bytes accessed | tf_op | source)
XLA Modules:
  0.0 466.1 jit_solution(16336467388483317776)
XLA Ops:
  7.2 1.7 pad_maximum_fusion.1
  8.9 3.8 copy.86
  12.7 8.5 %all-to-all-start.1 = ((bf16[2,128,4096]{1,0,2:T(2,128)(2,1)}), bf16[2,128,4096]{1,0,2:T(2,128)(2,1)}, u32[]{:S(2)}, u32[]{:S(2)}) async-start(bf16[2,128,4096]{1,0,2:T(2,128)(2,1)} %copy.86), calls=%async_computation.1 | async-start | bytes 4194304 | tf_op jit(solution)/shard_map/all_to_all | solution.py:17
  21.2 2.8 copy.82
  24.0 5.5 %copy.83 = bf16[1,128,4096]{1,0,2:T(2,128)(2,1)} copy(bf16[1,128,4096]{2,1,0:T(8,128)(2,1)} %param.15) | data formatting | bytes 2097152 | tf_op args[7]
  29.5 6.4 %pad_maximum_fusion = bf16[2,128,4096]{1,0,2:T(2,128)(2,1)} fusion(bf16[1,128,4096]{1,0,2:T(2,128)(2,1)} %copy.83, bf16[1,128,4096]{1,0,2:T(2,128)(2,1)S(1)} %copy.82), kind=kLoop, calls=%fused_computation.9 | loop fusion | flops 4194304 | bytes 4194304 | tf_op jit(solution)/shard_map/concatenate | solution.py:14
  35.9 15.9 %all-to-all-done.1 = bf16[2,128,4096]{1,0,2:T(2,128)(2,1)} async-done(((bf16[2,128,4096]{1,0,2:T(2,128)(2,1)}), bf16[2,128,4096]{1,0,2:T(2,128)(2,1)}, u32[]{:S(2)}, u32[]{:S(2)}) %all-to-all-start.1) | async-done | bytes 2097184 | tf_op jit(solution)/shard_map/all_to_all | solution.py:17
  51.9 4.4 all-to-all-start
  56.3 4.7 %copy.87 = bf16[2,128,8,512]{3,1,2,0:T(8,128)(2,1)S(1)} copy(bf16[2,128,8,512]{1,0,3,2:T(2,128)(2,1)} %bitcast.3) | data formatting | bytes 4194304 | tf_op jit(solution)/shard_map/all_to_all | solution.py:17
  61.2 1.9 copy-done.2
  67.0 3.1 multiply_convert_fusion.5
  70.1 1.7 convolution_bitcast_fusion.6
  73.1 1.7 convolution_bitcast_fusion.8
  74.9 11.1 %all-to-all-done = bf16[2,128,4096]{1,0,2:T(2,128)(2,1)} async-done(((bf16[2,128,4096]{1,0,2:T(2,128)(2,1)}), bf16[2,128,4096]{1,0,2:T(2,128)(2,1)}, u32[]{:S(2)}, u32[]{:S(2)}) %all-to-all-start) | async-done | bytes 2097184 | tf_op jit(solution)/shard_map/all_to_all | solution.py:17
  86.1 1.9 copy.84
  90.7 3.0 convolution_bitcast_fusion.7
  93.7 47.6 %all-reduce.15.cloned.1.call-done = (f32[1,512,512]{2,1,0:T(8,128)}, f32[1,512,512]{2,1,0:T(8,128)}) async-done(((f32[1,512,512]{2,1,0:T(8,128)}, f32[1,512,512]{2,1,0:T(8,128)}), (f32[1,512,512]{2,1,0:T(8,128)}, f32[1,512,512]{2,1,0:T(8,128)})) %all-reduce.15.cloned.1.call-update) | async-done | bytes 2097168 | tf_op jit(solution)/shard_map/psum | solution.py:159
  141.4 2.5 multiply_reduce_fusion.3
  145.5 2.3 multiply_convert_fusion.2
  148.8 1.7 convolution_bitcast_fusion.4
  151.0 65.0 %all-reduce.13.cloned.1.call-done = (f32[1,512,512]{2,1,0:T(8,128)}, f32[1,512,512]{2,1,0:T(8,128)}) async-done(((f32[1,512,512]{2,1,0:T(8,128)}, f32[1,512,512]{2,1,0:T(8,128)}), (f32[1,512,512]{2,1,0:T(8,128)}, f32[1,512,512]{2,1,0:T(8,128)})) %all-reduce.13.cloned.1.call-update) | async-done | bytes 2097168 | tf_op jit(solution)/shard_map/psum | solution.py:159
  216.0 2.4 multiply_reduce_fusion.1
  218.9 2.8 multiply_convert_fusion.3
  221.7 1.7 convolution_bitcast_fusion.5
  223.4 2.1 fusion.47
  225.5 1.8 convolution_bitcast_fusion.3
  227.3 2.7 fusion.12
  230.0 3.0 copy.101
  233.5 9.0 %reduce.9 = bf16[1024,512]{1,0:T(8,128)(2,1)} reduce(bf16[1024,1,512]{2,1,0:T(2,128)(2,1)} %bitcast.164, bf16[]{:T(256)} %broadcast.129), dimensions={1}, to_apply=%bitcast.149.reduce_sub_computation | reduce | bytes 2097154
  242.5 2.8 reshape.255
  245.3 6.6 %all-to-all-start.2 = ((bf16[8,2,32768]{2,1,0:T(2,128)(2,1)}), bf16[8,2,32768]{2,1,0:T(2,128)(2,1)}, u32[]{:S(2)}, u32[]{:S(2)}) async-start(bf16[8,2,32768]{2,1,0:T(2,128)(2,1)} %reshape.255), calls=%async_computation.2 | async-start | bytes 2097152 | tf_op jit(solution)/shard_map/all_to_all | solution.py:177
  251.9 1.5 fusion.27
  253.4 2.1 fusion.62
  255.5 2.1 fusion.60
  257.6 35.6 %all-reduce.11.cloned.1.call-done = (f32[1,512,512]{2,1,0:T(8,128)}, f32[1,512,512]{2,1,0:T(8,128)}) async-done(((f32[1,512,512]{2,1,0:T(8,128)}, f32[1,512,512]{2,1,0:T(8,128)}), (f32[1,512,512]{2,1,0:T(8,128)}, f32[1,512,512]{2,1,0:T(8,128)})) %all-reduce.11.cloned.1.call-update) | async-done | bytes 2097168 | tf_op jit(solution)/shard_map/psum | solution.py:178
  293.1 1.5 multiply_reduce_fusion.2
  301.4 2.6 add_convert_fusion.2
  309.8 3.5 copy.93
  313.3 1.6 fusion.17
  314.9 6.7 %all-to-all-start.3 = ((bf16[2,1024,512]{2,0,1:T(2,128)(2,1)}), bf16[2,1024,512]{2,0,1:T(2,128)(2,1)}, u32[]{:S(2)}, u32[]{:S(2)}) async-start(bf16[2,1024,512]{2,0,1:T(2,128)(2,1)} %copy.93), calls=%async_computation.3 | async-start | bytes 4194304 | tf_op jit(solution)/shard_map/all_to_all | solution.py:17
  321.7 3.9 fusion.18
  325.7 1.7 fusion.19
  327.4 64.3 %all-reduce.17.cloned.1.call-done = (bf16[1,512,512]{2,1,0:T(8,128)(2,1)}, bf16[1,512,512]{2,1,0:T(8,128)(2,1)}, bf16[1,512,512]{2,1,0:T(8,128)(2,1)}) async-done(((bf16[1,512,512]{2,1,0:T(8,128)(2,1)}, bf16[1,512,512]{2,1,0:T(8,128)(2,1)}, bf16[1,512,512]{2,1,0:T(8,128)(2,1)}), (bf16[1,512,512]{2,1,0:T(8,128)(2,1)}, bf16[1,512,512]{2,1,0:T(8,128)(2,1)}, ...) | async-done | bytes 1572880 | tf_op jit(solution)/shard_map/psum | solution.py:212
  391.8 4.5 reshape.256
  399.2 5.6 %fusion.55 = (bf16[1,128,8,512]{3,0,1,2:T(2,128)(2,1)S(1)}, bf16[1,128,8,512]{3,0,1,2:T(2,128)(2,1)S(1)}) fusion(bf16[2,128,8,512]{3,0,1,2:T(2,128)(2,1)} %bitcast.33), kind=kLoop, calls=%fused_computation.110 | loop fusion | bytes 4194304 | tf_op jit(solution)/shard_map/split | solution.py:16
  409.7 44.2 %all-reduce.19.cloned.1.call-done = (bf16[1,512,512]{2,1,0:T(8,128)(2,1)}, bf16[1,512,512]{2,1,0:T(8,128)(2,1)}, bf16[1,512,512]{2,1,0:T(8,128)(2,1)}) async-done(((bf16[1,512,512]{2,1,0:T(8,128)(2,1)}, bf16[1,512,512]{2,1,0:T(8,128)(2,1)}, bf16[1,512,512]{2,1,0:T(8,128)(2,1)}), (bf16[1,512,512]{2,1,0:T(8,128)(2,1)}, bf16[1,512,512]{2,1,0:T(8,128)(2,1)}, ...) | async-done | bytes 1572880 | tf_op jit(solution)/shard_map/psum | solution.py:212
  453.9 2.2 convert_element_type.196
  456.1 2.1 convert_element_type.198
  (136 shorter events, 33.5 us)
Async XLA Ops:
  12.7 8.5 %copy-start.43 = (f32[1,1,1024]{2,1,0:T(1,128)S(1)}, f32[1,1,1024]{2,1,0:T(1,128)}, u32[]{:S(2)}) copy-start(f32[1,1,1024]{2,1,0:T(1,128)} %param.11) | copy-start | bytes 12292
  12.7 8.5 %copy-start.31 = (bf16[1,128,4096]{2,1,0:T(8,128)(2,1)S(1)}, bf16[1,128,4096]{2,1,0:T(8,128)(2,1)}, u32[]{:S(2)}) copy-start(bf16[1,128,4096]{2,1,0:T(8,128)(2,1)} %param.8) | copy-start | bytes 3145732
  12.7 39.2 %all-to-all-start.1 = ((bf16[2,128,4096]{1,0,2:T(2,128)(2,1)}), bf16[2,128,4096]{1,0,2:T(2,128)(2,1)}, u32[]{:S(2)}, u32[]{:S(2)}) async-start(bf16[2,128,4096]{1,0,2:T(2,128)(2,1)} %copy.86), calls=%async_computation.1 | async-start | bytes 4194304 | tf_op jit(solution)/shard_map/all_to_all | solution.py:17
  51.9 34.2 %all-to-all-start = ((bf16[2,128,4096]{1,0,2:T(2,128)(2,1)}), bf16[2,128,4096]{1,0,2:T(2,128)(2,1)}, u32[]{:S(2)}, u32[]{:S(2)}) async-start(bf16[2,128,4096]{1,0,2:T(2,128)(2,1)} %pad_maximum_fusion), calls=%async_computation | async-start | bytes 4194304 | tf_op jit(solution)/shard_map/all_to_all | solution.py:17
  56.2 85.1 %all-reduce.15.cloned.1.call-start = ((), (), s32[]{:S(2)}) async-start(), calls=%async_computation.6 | async-start | bytes 4194304 | tf_op jit(solution)/shard_map/psum | solution.py:159
  61.0 10.8 %copy-start = (bf16[2,128,8,512]{3,1,2,0:T(8,128)(2,1)}, bf16[2,128,8,512]{3,1,2,0:T(8,128)(2,1)S(1)}, u32[]{:S(2)}) copy-start(bf16[2,128,8,512]{3,1,2,0:T(8,128)(2,1)S(1)} %copy.87) | copy-start | bytes 6291460
  61.0 2.0 copy-start.2
  63.0 1.2 copy-start.7
  64.2 1.4 copy-start.25
  65.0 5.2 %copy-start.27 = (f32[1024,512]{1,0:T(8,128)}, f32[1024,512]{1,0:T(8,128)S(1)}, u32[]{:S(2)}) copy-start(f32[1024,512]{1,0:T(8,128)S(1)} %fusion.37) | copy-start | bytes 6291460
  65.0 2.0 copy-start.15
  65.3 4.8 %copy-start.38 = (bf16[1,8,128,512]{3,2,1,0:T(8,128)(2,1)}, bf16[1,8,128,512]{3,2,1,0:T(8,128)(2,1)S(1)}, u32[]{:S(2)}) copy-start(bf16[1,8,128,512]{3,2,1,0:T(8,128)(2,1)S(1)} %fusion.7) | copy-start | bytes 3145732
  70.1 1.7 copy-start.34
  70.1 2.0 copy-start.32
  74.9 141.2 %all-reduce.13.cloned.1.call-start = ((), (), s32[]{:S(2)}) async-start(), calls=%async_computation.5 | async-start | bytes 4194304 | tf_op jit(solution)/shard_map/psum | solution.py:159
  90.7 50.7 %copy-start.8 = (f32[1,512,512]{2,1,0:T(8,128)S(1)}, f32[1,512,512]{2,1,0:T(8,128)}, u32[]{:S(2)}) copy-start(f32[1,512,512]{2,1,0:T(8,128)} %param.12) | copy-start | bytes 3145732
  141.4 2.5 copy-start.22
  143.9 1.6 copy-start.40
  144.6 3.2 copy-start.29
  150.5 142.6 %all-reduce.11.cloned.1.call-start = ((), (), s32[]{:S(2)}) async-start(), calls=%async_computation.4 | async-start | bytes 4194304 | tf_op jit(solution)/shard_map/psum | solution.py:178
  216.0 2.4 copy-start.23
  216.0 2.9 copy-start.30
  223.4 2.1 copy-start.41
  245.3 69.7 %all-to-all-start.2 = ((bf16[8,2,32768]{2,1,0:T(2,128)(2,1)}), bf16[8,2,32768]{2,1,0:T(2,128)(2,1)}, u32[]{:S(2)}, u32[]{:S(2)}) async-start(bf16[8,2,32768]{2,1,0:T(2,128)(2,1)} %reshape.255), calls=%async_computation.2 | async-start | bytes 2097152 | tf_op jit(solution)/shard_map/all_to_all | solution.py:177
  253.4 2.1 copy-start.36
  293.1 1.5 copy-start.12
  295.0 1.2 copy-start.35
  295.0 4.7 %copy-start.44 = (f32[1024,512]{1,0:T(8,128)S(1)}, f32[1024,512]{1,0:T(8,128)}, u32[]{:S(2)}) copy-start(f32[1024,512]{1,0:T(8,128)} %get-tuple-element.62) | copy-start | bytes 6291460
  296.2 1.5 copy-start.14
  297.7 1.9 copy-start.39
  298.0 1.9 copy-start.26
  298.1 2.5 copy-start.28
  298.9 2.5 copy-start.24
  301.4 2.7 copy-start.9
  304.1 3.6 copy-start.21
  304.1 2.0 copy-start.3
  304.1 2.6 copy-start.17
  306.8 1.6 copy-start.1
  306.8 1.9 copy-start.16
  309.7 3.5 copy-start.11
  314.9 6.8 %copy-start.6 = (f32[1,512,512]{2,1,0:T(8,128)S(1)}, f32[1,512,512]{2,1,0:T(8,128)}, u32[]{:S(2)}) copy-start(f32[1,512,512]{2,1,0:T(8,128)} %copy-done.4) | copy-start | bytes 3145732
  314.9 84.3 %all-to-all-start.3 = ((bf16[2,1024,512]{2,0,1:T(2,128)(2,1)}), bf16[2,1024,512]{2,0,1:T(2,128)(2,1)}, u32[]{:S(2)}, u32[]{:S(2)}) async-start(bf16[2,1024,512]{2,0,1:T(2,128)(2,1)} %copy.93), calls=%async_computation.3 | async-start | bytes 4194304 | tf_op jit(solution)/shard_map/all_to_all | solution.py:17
  321.7 70.1 %all-reduce.17.cloned.1.call-start = ((), (), s32[]{:S(2)}) async-start(), calls=%async_computation.7 | async-start | bytes 3145728 | tf_op jit(solution)/shard_map/psum | solution.py:212
  321.7 4.0 copy-start.10
  321.7 4.0 copy-start.13
  321.7 3.9 copy-start.20
  327.4 126.5 %all-reduce.19.cloned.1.call-start = ((), (), s32[]{:S(2)}) async-start(), calls=%async_computation.8 | async-start | bytes 3145728 | tf_op jit(solution)/shard_map/psum | solution.py:212
  453.9 4.4 copy-start.42
  (6 other events, 6.4 us)
Sparse Core Ops, SparseCore 0:
  75.0 66.3 all-reduce.14
  150.6 65.3 all-reduce.12
  227.4 65.6 all-reduce.10
  327.5 64.2 all-reduce.16
  394.2 59.5 all-reduce.18
